TPU v7x, 128 devices: a whole 4x4x4 slice. The times are simulated.
128 devices in a mesh: rows: 16 (over y, x), cols: 8 (over z, core).
Axes of the slice: x: 4, y: 4, z: 4, core: 2. Of those that a mesh axis runs over, the one named last changes fastest.
Arguments:
- ensemble: bfloat16 [64, 768, 1024], P(None, 'rows', 'cols'), may hold values from -6 to 6
- row_profile: bfloat16 [768, 16384], P('rows'), may hold values from 0.0072021484 to 0.071777344
- col_profile: bfloat16 [1024, 16384], P('cols'), may hold values from 0.006225586 to 0.0625
- obs_owned: float32 [128, 384], P(('rows', 'cols')), may hold values from -18 to 18
- noise_owned: float32 [128, 384], P(('rows', 'cols')), may hold values from 40.96 to 409.6
- block_owner: int32 [128], replicated, may hold values from 0 to 127, as said below
Outputs:
- updated: bfloat16 [64, 768, 1024], P(None, 'rows', 'cols')
Inputs may be any that keep to these rules, and one draw needn't show every extreme that they name: `block_owner`: each of the 128 devices owns at most 3 detector blocks, and some devices own exactly 3, some own 1 and some own none.
All inputs are finite; a program needn't handle non-finite values.
Results may differ from a plain program's by a relative error of at most 0.0011.
Values sent between devices are 32-bit elements; how exact they have to be, the bound alone decides.
A program may use at most 128 MiB of HBM per device.

v0:
```python
import math
import jax
import jax.numpy as jnp
from jax import lax
from jax.sharding import PartitionSpec as P

MEMBERS = 64
BLOCK = 128
CAP = 3


def partial_blocks(flat_field, row_prof, col_prof, first_block, block_count):
    group_size = math.gcd(block_count, 8)
    group_count = block_count // group_size
    span_cols = group_size * BLOCK
    local_rows = row_prof.shape[0]

    def group_terms(step_at):
        first_col = (first_block + step_at * group_size) * BLOCK
        col_part = lax.dynamic_slice_in_dim(col_prof, first_col, span_cols, 1)
        row_part = lax.dynamic_slice_in_dim(row_prof, first_col, span_cols, 1).astype(jnp.float32)
        along_cols = jnp.dot(flat_field, col_part, preferred_element_type=jnp.float32)
        along_cols = along_cols.reshape(MEMBERS, local_rows, span_cols)
        summed = jnp.sum(along_cols * row_part[None], axis=1)
        return summed.reshape(MEMBERS, group_size, BLOCK).transpose(1, 0, 2)

    terms = lax.map(group_terms, jnp.arange(group_count, dtype=jnp.int32))
    return terms.reshape(block_count, MEMBERS, BLOCK)


def member_stats(predictions, observed, weights):
    member_mean = jnp.mean(predictions, axis=1, keepdims=True)
    anomalies = (predictions - member_mean) / math.sqrt(MEMBERS - 1)
    residuals = observed[:, None, :] - predictions
    scaled = anomalies * weights[:, None, :]
    spread_mat = jnp.einsum("sjd,skd->jk", scaled, anomalies, precision=lax.Precision.HIGHEST)
    innovation = jnp.einsum("sjd,skd->jk", scaled, residuals, precision=lax.Precision.HIGHEST)
    return (spread_mat, innovation)


def on_device(ensemble, row_profile, col_profile, obs_owned, noise_owned, block_owner):
    own_index = lax.axis_index(("rows", "cols"))
    devices = lax.axis_size(("rows", "cols"))
    blocks = col_profile.shape[1] // BLOCK
    local_rows = ensemble.shape[1]
    local_cols = ensemble.shape[2]
    flat_field = ensemble.reshape(MEMBERS * local_rows, local_cols)
    block_index = jnp.arange(blocks, dtype=jnp.int32)
    same_owner = block_owner[None, :] == block_owner[:, None]
    earlier = block_index[None, :] < block_index[:, None]
    slot_rank = jnp.sum((same_owner & earlier).astype(jnp.int32), axis=1)
    obs_slots = obs_owned.reshape(CAP, BLOCK)
    noise_slots = noise_owned.reshape(CAP, BLOCK)
    partials = partial_blocks(flat_field, row_profile, col_profile, 0, blocks)
    owner_grid = jnp.arange(devices, dtype=jnp.int32)[:, None, None]
    slot_grid = jnp.arange(CAP, dtype=jnp.int32)[None, :, None]
    slot_hit = (block_owner[None, None, :] == owner_grid) & (slot_rank[None, None, :] == slot_grid)
    slot_valid = jnp.any(slot_hit, axis=2)
    slot_block = jnp.sum(jnp.where(slot_hit, block_index[None, None, :], 0), axis=2)
    send_buffer = jnp.where(slot_valid[:, :, None, None], partials[slot_block], 0.0)
    predictions = jnp.sum(
        lax.all_to_all(send_buffer, ("rows", "cols"), split_axis=0, concat_axis=0, tiled=True),
        axis=0,
    )
    owned_count = jnp.sum((block_owner == own_index).astype(jnp.int32))
    live_slot = jnp.arange(CAP, dtype=jnp.int32) < owned_count
    weights = jnp.where(live_slot[:, None], 1.0 / noise_slots, 0.0)
    spread_mat, innovation = member_stats(predictions, obs_slots, weights)
    spread_mat, innovation = lax.psum((spread_mat, innovation), ("rows", "cols"))
    eye_mat = jnp.eye(MEMBERS, dtype=jnp.float32)
    factor = jnp.linalg.cholesky(eye_mat + spread_mat)
    gain_weights = jax.scipy.linalg.cho_solve((factor, True), innovation)
    field_flat = ensemble.astype(jnp.float32).reshape(MEMBERS, -1)
    member_mean = jnp.mean(field_flat, axis=0, keepdims=True)
    anomalies = (field_flat - member_mean) / math.sqrt(MEMBERS - 1)
    moved = field_flat + jnp.dot(gain_weights.T, anomalies, precision=lax.Precision.HIGHEST)
    return moved.reshape(ensemble.shape).astype(jnp.bfloat16)


def solution(mesh):
    in_specs = (
        P(None, "rows", "cols"),
        P("rows", None),
        P("cols", None),
        P(("rows", "cols"), None),
        P(("rows", "cols"), None),
        P(),
    )
    out_specs = P(None, "rows", "cols")
    return jax.shard_map(
        on_device, mesh=mesh, in_specs=in_specs, out_specs=out_specs, check_vma=False
    )
```

profile of v0, /device:TPU:1, one launch (start us, length us, event | category | flops | bytes accessed | tf_op | source)
XLA Modules:
  0.0 768.0 jit_solution(12466156515473649168)
XLA Ops:
  1.9 479.6 %while.12 = (s32[]{:T(128)}, f32[16,8,64,128]{3,2,1,0:T(8,128)}, s32[16]{0:T(128)S(1)}, bf16[128,16384]{1,0:T(8,128)(2,1)}, bf16[3072,128]{1,0:T(8,128)(2,1)}, /...) while((s32[]{:T(128)}, f32[16,8,64,128]{3,2,1,0:T(8,128)}, ...), condition=%wide.region_4.5_spmd, body=%wide.region_2.4_spmd.sunk | while | flops 811581440 | bytes 53182640 | solution.py:27
  10.9 12.6 %copy.39 = f32[3072,1024]{1,0:T(8,128)} copy(f32[3072,1024]{0,1:T(8,128)} %convolution_bitcast_fusion.4) | data formatting | bytes 25165824 | tf_op jit(solution)/shard_map/while/body/eval_jaxpr/dot_general | solution.py:22
  40.9 12.6 %copy.39 = f32[3072,1024]{1,0:T(8,128)} copy(f32[3072,1024]{0,1:T(8,128)} %convolution_bitcast_fusion.4) | data formatting | bytes 25165824 | tf_op jit(solution)/shard_map/while/body/eval_jaxpr/dot_general | solution.py:22
  70.8 12.6 %copy.39 = f32[3072,1024]{1,0:T(8,128)} copy(f32[3072,1024]{0,1:T(8,128)} %convolution_bitcast_fusion.4) | data formatting | bytes 25165824 | tf_op jit(solution)/shard_map/while/body/eval_jaxpr/dot_general | solution.py:22
  100.8 12.6 %copy.39 = f32[3072,1024]{1,0:T(8,128)} copy(f32[3072,1024]{0,1:T(8,128)} %convolution_bitcast_fusion.4) | data formatting | bytes 25165824 | tf_op jit(solution)/shard_map/while/body/eval_jaxpr/dot_general | solution.py:22
  130.8 12.6 %copy.39 = f32[3072,1024]{1,0:T(8,128)} copy(f32[3072,1024]{0,1:T(8,128)} %convolution_bitcast_fusion.4) | data formatting | bytes 25165824 | tf_op jit(solution)/shard_map/while/body/eval_jaxpr/dot_general | solution.py:22
  160.8 12.6 %copy.39 = f32[3072,1024]{1,0:T(8,128)} copy(f32[3072,1024]{0,1:T(8,128)} %convolution_bitcast_fusion.4) | data formatting | bytes 25165824 | tf_op jit(solution)/shard_map/while/body/eval_jaxpr/dot_general | solution.py:22
  190.8 12.6 %copy.39 = f32[3072,1024]{1,0:T(8,128)} copy(f32[3072,1024]{0,1:T(8,128)} %convolution_bitcast_fusion.4) | data formatting | bytes 25165824 | tf_op jit(solution)/shard_map/while/body/eval_jaxpr/dot_general | solution.py:22
  220.7 12.6 %copy.39 = f32[3072,1024]{1,0:T(8,128)} copy(f32[3072,1024]{0,1:T(8,128)} %convolution_bitcast_fusion.4) | data formatting | bytes 25165824 | tf_op jit(solution)/shard_map/while/body/eval_jaxpr/dot_general | solution.py:22
  250.7 12.6 %copy.39 = f32[3072,1024]{1,0:T(8,128)} copy(f32[3072,1024]{0,1:T(8,128)} %convolution_bitcast_fusion.4) | data formatting | bytes 25165824 | tf_op jit(solution)/shard_map/while/body/eval_jaxpr/dot_general | solution.py:22
  280.7 12.6 %copy.39 = f32[3072,1024]{1,0:T(8,128)} copy(f32[3072,1024]{0,1:T(8,128)} %convolution_bitcast_fusion.4) | data formatting | bytes 25165824 | tf_op jit(solution)/shard_map/while/body/eval_jaxpr/dot_general | solution.py:22
  310.7 12.6 %copy.39 = f32[3072,1024]{1,0:T(8,128)} copy(f32[3072,1024]{0,1:T(8,128)} %convolution_bitcast_fusion.4) | data formatting | bytes 25165824 | tf_op jit(solution)/shard_map/while/body/eval_jaxpr/dot_general | solution.py:22
  340.6 12.6 %copy.39 = f32[3072,1024]{1,0:T(8,128)} copy(f32[3072,1024]{0,1:T(8,128)} %convolution_bitcast_fusion.4) | data formatting | bytes 25165824 | tf_op jit(solution)/shard_map/while/body/eval_jaxpr/dot_general | solution.py:22
  370.6 12.6 %copy.39 = f32[3072,1024]{1,0:T(8,128)} copy(f32[3072,1024]{0,1:T(8,128)} %convolution_bitcast_fusion.4) | data formatting | bytes 25165824 | tf_op jit(solution)/shard_map/while/body/eval_jaxpr/dot_general | solution.py:22
  392.9 7.6 convolution_bitcast_fusion.4
  400.6 12.6 %copy.39 = f32[3072,1024]{1,0:T(8,128)} copy(f32[3072,1024]{0,1:T(8,128)} %convolution_bitcast_fusion.4) | data formatting | bytes 25165824 | tf_op jit(solution)/shard_map/while/body/eval_jaxpr/dot_general | solution.py:22
  430.5 12.6 %copy.39 = f32[3072,1024]{1,0:T(8,128)} copy(f32[3072,1024]{0,1:T(8,128)} %convolution_bitcast_fusion.4) | data formatting | bytes 25165824 | tf_op jit(solution)/shard_map/while/body/eval_jaxpr/dot_general | solution.py:22
  452.9 7.6 convolution_bitcast_fusion.4
  460.5 12.6 %copy.39 = f32[3072,1024]{1,0:T(8,128)} copy(f32[3072,1024]{0,1:T(8,128)} %convolution_bitcast_fusion.4) | data formatting | bytes 25165824 | tf_op jit(solution)/shard_map/while/body/eval_jaxpr/dot_general | solution.py:22
  482.0 8.1 %gather_fusion = f32[384,64,128]{2,1,0:T(8,128)} fusion(f32[128,64,128]{2,1,0:T(8,128)} %bitcast.75, s32[1024]{0:T(1024)S(1)} %pad_clamp_fusion), kind=kCustom, calls=%fused_computation | custom fusion | bytes 25167360 | tf_op jit(solution)/shard_map/gather | solution.py:60
  490.1 10.2 %broadcast_select_fusion = f32[128,3,64,128]{3,2,1,0:T(8,128)} fusion(f32[128,3,64,128]{3,2,1,0:T(8,128)} %bitcast.71, pred[128,3]{1,0:T(8,128)(4,1)S(1)} %copy.15), kind=kLoop, calls=%fused_computation.9 | loop fusion | flops 3145728 | bytes 25166208 | tf_op jit(solution)/shard_map/jit(_where)/select_n | solution.py:60
  500.3 11.9 %all-to-all-start = ((f32[128,3,64,128]{3,2,1,0:T(8,128)}), f32[128,3,64,128]{3,2,1,0:T(8,128)}, u32[]{:S(2)}, u32[]{:S(2)}) async-start(f32[128,3,64,128]{3,2,1,0:T(8,128)} %broadcast_select_fusion), calls=%async_computation | async-start | bytes 25165824 | tf_op jit(solution)/shard_map/all_to_all | solution.py:62
  514.0 160.1 %all-to-all-done = f32[128,3,64,128]{3,2,1,0:T(8,128)} async-done(((f32[128,3,64,128]{3,2,1,0:T(8,128)}), f32[128,3,64,128]{3,2,1,0:T(8,128)}, u32[]{:S(2)}, u32[]{:S(2)}) %all-to-all-start) | async-done | bytes 12582944 | tf_op jit(solution)/shard_map/all_to_all | solution.py:62
  681.0 70.9 %all-reduce = (f32[64,64]{1,0:T(8,128)S(1)}, f32[64,64]{1,0:T(8,128)S(1)}) all-reduce(f32[64,64]{1,0:T(8,128)S(1)} %convolution_bitcast_fusion.1, f32[64,64]{1,0:T(8,128)S(1)} %convolution_bitcast_fusion.2), channel_id=1, replica_groups=mesh['rows'=16,'cols'=8] {'rows','cols'}, use_global_device_ids=true, to_apply=%region_12.13 | all-reduce | flops 8192 | bytes 65536 | tf_op jit(solution)/shard_map/psum | solution.py:69
  (138 shorter events, 278.2 us)
Async XLA Ops:
  500.3 11.9 %copy-start = (bf16[3072,128]{1,0:T(8,128)(2,1)S(1)}, bf16[3072,128]{1,0:T(8,128)(2,1)}, u32[]{:S(2)}) copy-start(bf16[3072,128]{1,0:T(8,128)(2,1)} %get-tuple-element.174) | copy-start | bytes 2359300
  500.3 12.1 %copy-start.2 = (f32[1,384]{1,0:T(1,128)S(1)}, f32[1,384]{1,0:T(1,128)}, u32[]{:S(2)}) copy-start(f32[1,384]{1,0:T(1,128)} %param.11) | copy-start | bytes 4612
  500.3 12.1 %copy-start.3 = (s32[128]{0:T(128)S(1)}, s32[128]{0:T(128)}, u32[]{:S(2)}) copy-start(s32[128]{0:T(128)} %param.13) | copy-start | bytes 1540
  500.3 13.4 %copy-start.1 = (f32[1,384]{1,0:T(1,128)S(1)}, f32[1,384]{1,0:T(1,128)}, u32[]{:S(2)}) copy-start(f32[1,384]{1,0:T(1,128)} %param.12) | copy-start | bytes 4612
  500.3 173.8 %all-to-all-start = ((f32[128,3,64,128]{3,2,1,0:T(8,128)}), f32[128,3,64,128]{3,2,1,0:T(8,128)}, u32[]{:S(2)}, u32[]{:S(2)}) async-start(f32[128,3,64,128]{3,2,1,0:T(8,128)} %broadcast_select_fusion), calls=%async_computation | async-start | bytes 25165824 | tf_op jit(solution)/shard_map/all_to_all | solution.py:62
where the time goes:
time: 772 us; the launch traced here: 768 us
  local copies, waits for them, and re-layouts  235 us (30%)
  waiting for transfers between devices  160 us (21%)
  other arithmetic  153 us (20%)
  matrix products  125 us (16%)
  blocking collectives  70.9 us (9%)
  starting transfers between devices  11.9 us (2%)
  loops' own time  11.5 us (1%)
    dot_general x16, local copies, waits for them, and re-layouts, group_terms(): jnp.dot(flat_field, col_part, preferred_element_type=jnp.float32)  201 us
    all_to_all x1, waiting for transfers between devices, on_device(): lax.all_to_all(send_buffer, ('rows', 'cols'), split_axis=0, concat_axis=0...  160 us
    dot_general x16, matrix products, group_terms(): jnp.dot(flat_field, col_part, preferred_element_type=jnp.float32)  122 us
    reduce_sum x16, other arithmetic, group_terms(): summed = jnp.sum(along_cols * row_part[None], axis=1)  106 us
    psum x1, blocking collectives, on_device(): lax.psum((spread_mat, innovation), ('rows', 'cols'))  70.9 us
  transfers between devices with their start and end apart: 1, of which 1 were waited for; matrix products, arithmetic and copies ran while one was open for 0% of the time, Pallas kernels for 0%

commit v1 on v0

--- a/solution.py
+++ b/solution.py
@@ -66,7 +66,8 @@
     live_slot = jnp.arange(CAP, dtype=jnp.int32) < owned_count
     weights = jnp.where(live_slot[:, None], 1.0 / noise_slots, 0.0)
     spread_mat, innovation = member_stats(predictions, obs_slots, weights)
-    spread_mat, innovation = lax.psum((spread_mat, innovation), ("rows", "cols"))
+    change_types_now = lambda m: lax.psum(lax.psum(m, axis_name="rows"), "cols")
+    spread_mat, innovation = change_types_now((spread_mat, innovation))
     eye_mat = jnp.eye(MEMBERS, dtype=jnp.float32)
     factor = jnp.linalg.cholesky(eye_mat + spread_mat)
     gain_weights = jax.scipy.linalg.cho_solve((factor, True), innovation)

time: 772 us -> 802 us (1.039)
  blocking collectives: 70.9 us -> 99.2 us
    psum x1 -> x2, blocking collectives: 70.9 us -> 99.2 us  [on_device(): change_types_now = lambda m: lax.psum(lax.psum(m, axis_name='rows'), 'cols')]
where the time goes in v1:
time: 802 us; the launch traced here: 796 us
  local copies, waits for them, and re-layouts  235 us (29%)
  waiting for transfers between devices  160 us (20%)
  other arithmetic  153 us (19%)
  matrix products  125 us (16%)
  blocking collectives  99.2 us (12%)
  starting transfers between devices  11.9 us (1%)
  loops' own time  11.5 us (1%)
    dot_general x16, local copies, waits for them, and re-layouts, group_terms(): jnp.dot(flat_field, col_part, preferred_element_type=jnp.float32)  201 us
    all_to_all x1, waiting for transfers between devices, on_device(): lax.all_to_all(send_buffer, ('rows', 'cols'), split_axis=0, concat_axis=0...  160 us
    dot_general x16, matrix products, group_terms(): jnp.dot(flat_field, col_part, preferred_element_type=jnp.float32)  122 us
    reduce_sum x16, other arithmetic, group_terms(): summed = jnp.sum(along_cols * row_part[None], axis=1)  106 us
    psum x2, blocking collectives, on_device(): change_types_now = lambda m: lax.psum(lax.psum(m, axis_name='rows'), 'cols')  99.2 us
  transfers between devices with their start and end apart: 1, of which 1 were waited for; matrix products, arithmetic and copies ran while one was open for 0% of the time, Pallas kernels for 0%

profile of v1, /device:TPU:1, one launch (start us, length us, event | category | flops | bytes accessed | tf_op | source)
XLA Modules:
  0.0 796.3 jit_solution(9917908438308344663)
XLA Ops:
  1.9 479.6 %while.12 = (s32[]{:T(128)}, f32[16,8,64,128]{3,2,1,0:T(8,128)}, s32[16]{0:T(128)S(1)}, bf16[128,16384]{1,0:T(8,128)(2,1)}, bf16[3072,128]{1,0:T(8,128)(2,1)}, /...) while((s32[]{:T(128)}, f32[16,8,64,128]{3,2,1,0:T(8,128)}, ...), condition=%wide.region_4.5_spmd, body=%wide.region_2.4_spmd.sunk | while | flops 811581440 | bytes 53182640 | solution.py:27
  10.9 12.6 %copy.39 = f32[3072,1024]{1,0:T(8,128)} copy(f32[3072,1024]{0,1:T(8,128)} %convolution_bitcast_fusion.4) | data formatting | bytes 25165824 | tf_op jit(solution)/shard_map/while/body/eval_jaxpr/dot_general | solution.py:22
  40.9 12.6 %copy.39 = f32[3072,1024]{1,0:T(8,128)} copy(f32[3072,1024]{0,1:T(8,128)} %convolution_bitcast_fusion.4) | data formatting | bytes 25165824 | tf_op jit(solution)/shard_map/while/body/eval_jaxpr/dot_general | solution.py:22
  70.8 12.6 %copy.39 = f32[3072,1024]{1,0:T(8,128)} copy(f32[3072,1024]{0,1:T(8,128)} %convolution_bitcast_fusion.4) | data formatting | bytes 25165824 | tf_op jit(solution)/shard_map/while/body/eval_jaxpr/dot_general | solution.py:22
  100.8 12.6 %copy.39 = f32[3072,1024]{1,0:T(8,128)} copy(f32[3072,1024]{0,1:T(8,128)} %convolution_bitcast_fusion.4) | data formatting | bytes 25165824 | tf_op jit(solution)/shard_map/while/body/eval_jaxpr/dot_general | solution.py:22
  130.8 12.6 %copy.39 = f32[3072,1024]{1,0:T(8,128)} copy(f32[3072,1024]{0,1:T(8,128)} %convolution_bitcast_fusion.4) | data formatting | bytes 25165824 | tf_op jit(solution)/shard_map/while/body/eval_jaxpr/dot_general | solution.py:22
  160.8 12.6 %copy.39 = f32[3072,1024]{1,0:T(8,128)} copy(f32[3072,1024]{0,1:T(8,128)} %convolution_bitcast_fusion.4) | data formatting | bytes 25165824 | tf_op jit(solution)/shard_map/while/body/eval_jaxpr/dot_general | solution.py:22
  190.8 12.6 %copy.39 = f32[3072,1024]{1,0:T(8,128)} copy(f32[3072,1024]{0,1:T(8,128)} %convolution_bitcast_fusion.4) | data formatting | bytes 25165824 | tf_op jit(solution)/shard_map/while/body/eval_jaxpr/dot_general | solution.py:22
  220.7 12.6 %copy.39 = f32[3072,1024]{1,0:T(8,128)} copy(f32[3072,1024]{0,1:T(8,128)} %convolution_bitcast_fusion.4) | data formatting | bytes 25165824 | tf_op jit(solution)/shard_map/while/body/eval_jaxpr/dot_general | solution.py:22
  250.7 12.6 %copy.39 = f32[3072,1024]{1,0:T(8,128)} copy(f32[3072,1024]{0,1:T(8,128)} %convolution_bitcast_fusion.4) | data formatting | bytes 25165824 | tf_op jit(solution)/shard_map/while/body/eval_jaxpr/dot_general | solution.py:22
  280.7 12.6 %copy.39 = f32[3072,1024]{1,0:T(8,128)} copy(f32[3072,1024]{0,1:T(8,128)} %convolution_bitcast_fusion.4) | data formatting | bytes 25165824 | tf_op jit(solution)/shard_map/while/body/eval_jaxpr/dot_general | solution.py:22
  310.7 12.6 %copy.39 = f32[3072,1024]{1,0:T(8,128)} copy(f32[3072,1024]{0,1:T(8,128)} %convolution_bitcast_fusion.4) | data formatting | bytes 25165824 | tf_op jit(solution)/shard_map/while/body/eval_jaxpr/dot_general | solution.py:22
  340.6 12.6 %copy.39 = f32[3072,1024]{1,0:T(8,128)} copy(f32[3072,1024]{0,1:T(8,128)} %convolution_bitcast_fusion.4) | data formatting | bytes 25165824 | tf_op jit(solution)/shard_map/while/body/eval_jaxpr/dot_general | solution.py:22
  370.6 12.6 %copy.39 = f32[3072,1024]{1,0:T(8,128)} copy(f32[3072,1024]{0,1:T(8,128)} %convolution_bitcast_fusion.4) | data formatting | bytes 25165824 | tf_op jit(solution)/shard_map/while/body/eval_jaxpr/dot_general | solution.py:22
  400.6 12.6 %copy.39 = f32[3072,1024]{1,0:T(8,128)} copy(f32[3072,1024]{0,1:T(8,128)} %convolution_bitcast_fusion.4) | data formatting | bytes 25165824 | tf_op jit(solution)/shard_map/while/body/eval_jaxpr/dot_general | solution.py:22
  430.5 12.6 %copy.39 = f32[3072,1024]{1,0:T(8,128)} copy(f32[3072,1024]{0,1:T(8,128)} %convolution_bitcast_fusion.4) | data formatting | bytes 25165824 | tf_op jit(solution)/shard_map/while/body/eval_jaxpr/dot_general | solution.py:22
  452.9 7.6 convolution_bitcast_fusion.4
  460.5 12.6 %copy.39 = f32[3072,1024]{1,0:T(8,128)} copy(f32[3072,1024]{0,1:T(8,128)} %convolution_bitcast_fusion.4) | data formatting | bytes 25165824 | tf_op jit(solution)/shard_map/while/body/eval_jaxpr/dot_general | solution.py:22
  482.0 8.1 %gather_fusion = f32[384,64,128]{2,1,0:T(8,128)} fusion(f32[128,64,128]{2,1,0:T(8,128)} %bitcast.75, s32[1024]{0:T(1024)S(1)} %pad_clamp_fusion), kind=kCustom, calls=%fused_computation | custom fusion | bytes 25167360 | tf_op jit(solution)/shard_map/gather | solution.py:60
  490.1 10.2 %broadcast_select_fusion = f32[128,3,64,128]{3,2,1,0:T(8,128)} fusion(f32[128,3,64,128]{3,2,1,0:T(8,128)} %bitcast.71, pred[128,3]{1,0:T(8,128)(4,1)S(1)} %copy.15), kind=kLoop, calls=%fused_computation.9 | loop fusion | flops 3145728 | bytes 25166208 | tf_op jit(solution)/shard_map/jit(_where)/select_n | solution.py:60
  500.3 11.9 %all-to-all-start = ((f32[128,3,64,128]{3,2,1,0:T(8,128)}), f32[128,3,64,128]{3,2,1,0:T(8,128)}, u32[]{:S(2)}, u32[]{:S(2)}) async-start(f32[128,3,64,128]{3,2,1,0:T(8,128)} %broadcast_select_fusion), calls=%async_computation | async-start | bytes 25165824 | tf_op jit(solution)/shard_map/all_to_all | solution.py:62
  514.0 160.1 %all-to-all-done = f32[128,3,64,128]{3,2,1,0:T(8,128)} async-done(((f32[128,3,64,128]{3,2,1,0:T(8,128)}), f32[128,3,64,128]{3,2,1,0:T(8,128)}, u32[]{:S(2)}, u32[]{:S(2)}) %all-to-all-start) | async-done | bytes 12582944 | tf_op jit(solution)/shard_map/all_to_all | solution.py:62
  681.0 58.5 %all-reduce = (f32[64,64]{1,0:T(8,128)S(1)}, f32[64,64]{1,0:T(8,128)S(1)}) all-reduce(f32[64,64]{1,0:T(8,128)S(1)} %convolution_bitcast_fusion.1, f32[64,64]{1,0:T(8,128)S(1)} %convolution_bitcast_fusion.2), channel_id=1, replica_groups=mesh['rows'=16,'cols'=8] {'rows'}, use_global_device_ids=true, to_apply=%region_13.14 | all-reduce | flops 8192 | bytes 65536 | tf_op jit(solution)/shard_map/psum | solution.py:69
  739.4 40.8 %all-reduce.1 = (f32[64,64]{1,0:T(8,128)S(1)}, f32[64,64]{1,0:T(8,128)S(1)}) all-reduce(f32[64,64]{1,0:T(8,128)S(1)} %get-tuple-element.103, f32[64,64]{1,0:T(8,128)S(1)} %get-tuple-element.104), channel_id=1, replica_groups=mesh['rows'=16,'cols'=8] {'cols'}, use_global_device_ids=true, to_apply=%region_14.15 | all-reduce | flops 8192 | bytes 65536 | tf_op jit(solution)/shard_map/psum | solution.py:69
  (139 shorter events, 285.8 us)
Async XLA Ops:
  500.3 11.9 %copy-start = (bf16[3072,128]{1,0:T(8,128)(2,1)S(1)}, bf16[3072,128]{1,0:T(8,128)(2,1)}, u32[]{:S(2)}) copy-start(bf16[3072,128]{1,0:T(8,128)(2,1)} %get-tuple-element.176) | copy-start | bytes 2359300
  500.3 12.1 %copy-start.2 = (f32[1,384]{1,0:T(1,128)S(1)}, f32[1,384]{1,0:T(1,128)}, u32[]{:S(2)}) copy-start(f32[1,384]{1,0:T(1,128)} %param.11) | copy-start | bytes 4612
  500.3 12.1 %copy-start.3 = (s32[128]{0:T(128)S(1)}, s32[128]{0:T(128)}, u32[]{:S(2)}) copy-start(s32[128]{0:T(128)} %param.13) | copy-start | bytes 1540
  500.3 13.4 %copy-start.1 = (f32[1,384]{1,0:T(1,128)S(1)}, f32[1,384]{1,0:T(1,128)}, u32[]{:S(2)}) copy-start(f32[1,384]{1,0:T(1,128)} %param.12) | copy-start | bytes 4612
  500.3 173.8 %all-to-all-start = ((f32[128,3,64,128]{3,2,1,0:T(8,128)}), f32[128,3,64,128]{3,2,1,0:T(8,128)}, u32[]{:S(2)}, u32[]{:S(2)}) async-start(f32[128,3,64,128]{3,2,1,0:T(8,128)} %broadcast_select_fusion), calls=%async_computation | async-start | bytes 25165824 | tf_op jit(solution)/shard_map/all_to_all | solution.py:62
